TPU v7x, 256 devices: a whole 4x4x8 slice. The times are simulated.
256 devices in a mesh: fib: 32 (over y, z), wav: 4 (over x), exp: 2 (over core).
Axes of the slice: x: 4, y: 4, z: 8, core: 2. Of those that a mesh axis runs over, the one named last changes fastest.
Arguments:
- pixels: float32 [8, 1920, 8192], P('exp', 'wav', 'fib'), may hold values from -6 to 6
- pixel_ivar: float32 [8, 1920, 8192], P('exp', 'wav', 'fib'), may hold values from 0.25 to 4
- clip_bits: int32 [8, 128, 8192], P('exp', 'wav', 'fib'), may hold values from 0 to 32767
- coupling: float32 [8192], P('fib'), may hold values from 0.5 to 200
- counts: int32 [8192], P('fib'), may hold values from 1 to 8
- good_flags: int32 [8, 8192], P('exp', 'fib'), may hold values 0 or 1
- owner_slot: int32 [8192], replicated, may hold values from 0 to 8191, as said below
Outputs:
- coadd_flux: float32 [1920, 8192], P(('wav', 'exp'), 'fib')
- coadd_ivar: float32 [1920, 8192], P(('wav', 'exp'), 'fib')
- coadd_res: float32 [3, 1920, 8192], P(None, ('wav', 'exp'), 'fib')
Inputs may be any that keep to these rules, and one draw needn't show every extreme that they name: A permutation of the fibres; fibre f belongs to coadd index owner_slot[f] // 256 of fib, and the 256 fibres of each index of fib go 8 to every coadd index.
All inputs are finite; a program needn't handle non-finite values. No bound on the sum of `good_flags` on one device may be relied on, other than what follows from the above.
Results may differ from a plain program's by a relative error of at most 0.0001.
Values sent between devices are 32-bit elements; how exact they have to be, the bound alone decides.
A program may use at most 128 MiB of HBM per device.

v0:
```python
import functools

import jax
import jax.numpy as jnp
from jax import lax
from jax.experimental import pallas as pl
from jax.experimental.pallas import tpu as pltpu
from jax.sharding import PartitionSpec as P

HALO = 50
BLOCKS = 8
BITS = 15
LANES = 128
HALVES = 2
F_DEV = LANES * HALVES
ROWS = 256
SLOT_ROW = 240

F32 = jnp.float32
BF16 = jnp.bfloat16


def pieces(x):
    high = x.astype(BF16)
    rest = x - high.astype(F32)
    middle = rest.astype(BF16)
    low = (rest - middle.astype(F32)).astype(BF16)
    return high, middle, low


def exact_dot(one_hot, x, dims, one_hot_first):
    total = None
    for piece in pieces(x):
        pair = (one_hot, piece) if one_hot_first else (piece, one_hot)
        part = lax.dot_general(*pair, (dims, ((), ())), preferred_element_type=F32)
        total = part if total is None else total + part
    return total


def exchange_kernel(
    n_fib,
    n_wav,
    pix_hbm,
    ivar_hbm,
    bits_hbm,
    coupling_ref,
    counts_ref,
    good_ref,
    slots_ref,
    got_a,
    got_b,
    pix,
    ivar,
    bits,
    weight,
    fac_m,
    fac_y,
    fac_q,
    sums,
    theirs,
    send_a,
    send_b,
    sort_ref,
    edge_out,
    edge_in,
    red,
    far,
    load_sem,
    edge_send,
    edge_recv,
    half_send,
    half_recv,
    a_send,
    a_recv,
    b_send,
    b_recv,
):
    fib, wav, exp = lax.axis_index("fib"), lax.axis_index("wav"), lax.axis_index("exp")
    e_dev = good_ref.shape[0]
    chains = e_dev * HALVES
    waves = ivar.shape[1]
    step_count = waves // BLOCKS
    words = bits.shape[1] // BLOCKS
    half = waves // 2
    per = F_DEV // n_fib

    loads = []

    def load(src, dst, rows, number):
        for chain in range(chains):
            e, h = chain // HALVES, chain % HALVES
            copy = pltpu.make_async_copy(
                src.at[e, :, pl.ds(h * LANES, LANES)], dst.at[chain], load_sem.at[number, chain]
            )
            copy.start()
            loads.append(copy)

    load(bits_hbm, bits, None, 0)
    load(ivar_hbm, ivar, None, 1)
    load(pix_hbm, pix, None, 2)

    def to(**where):
        return {"device_id": where, "device_id_type": pl.DeviceIdType.MESH}

    def fib_peer(k):
        return lax.rem(fib + k, n_fib)

    wav_right = lax.rem(wav + 1, n_wav)
    wav_left = lax.rem(wav + n_wav - 1, n_wav)
    partner = 1 - exp

    barrier = pltpu.get_barrier_semaphore()

    def greet(k, _):
        pl.semaphore_signal(barrier, inc=1, **to(fib=fib_peer(k)))
        return 0

    pl.semaphore_signal(barrier, inc=1, **to(exp=partner))
    pl.semaphore_signal(barrier, inc=1, **to(wav=wav_right))
    pl.semaphore_signal(barrier, inc=1, **to(wav=wav_left))
    lax.fori_loop(1, n_fib, greet, 0)

    slot_row = jnp.concatenate(
        [slots_ref[pl.ds(fib * HALVES + h, 1), :] for h in range(HALVES)], axis=1
    )
    owner = slot_row // F_DEV
    owned = owner == lax.broadcasted_iota(jnp.int32, (n_fib, F_DEV), 0)
    before = lax.broadcasted_iota(jnp.int32, (F_DEV, F_DEV), 0) < lax.broadcasted_iota(
        jnp.int32, (F_DEV, F_DEV), 1
    )
    one, zero = jnp.ones((), F32), jnp.zeros((), F32)
    earlier = jnp.dot(
        jnp.where(owned, one, zero).astype(BF16),
        jnp.where(before, one, zero).astype(BF16),
        preferred_element_type=F32,
    )
    rank = jnp.sum(jnp.where(owned, earlier, zero), axis=0, keepdims=True)
    place = owner.astype(F32) * float(per) + rank
    row_of = lax.broadcasted_iota(jnp.int32, (F_DEV, F_DEV), 0).astype(F32)
    sort_ref[...] = jnp.where(row_of == place, one, zero).astype(BF16)
    slot_f32 = (slot_row - owner * F_DEV).astype(F32)

    c = [jnp.broadcast_to(coupling_ref[pl.ds(h, 1), :], (BLOCKS, LANES)) for h in range(HALVES)]
    sublane = lax.broadcasted_iota(jnp.int32, (BLOCKS, LANES), 0)
    at_first = jnp.where((sublane == 0) & (wav == 0), one, zero)
    at_last = jnp.where((sublane == BLOCKS - 1) & (wav == n_wav - 1), one, zero)
    link_first = [2.0 * c[h] - c[h] * at_first for h in range(HALVES)]
    link_last = [2.0 * c[h] - c[h] * at_last for h in range(HALVES)]

    usable = []
    for chain in range(chains):
        e, h = chain // HALVES, chain % HALVES
        observed = (exp * e_dev + e) < counts_ref[pl.ds(h, 1), :]
        good = good_ref[pl.ds(e, 1), pl.ds(h * LANES, LANES)]
        usable.append(jnp.where(observed, good, 0) * ((1 << BITS) - 1))
    usable = [jnp.broadcast_to(u, (BLOCKS, LANES)) for u in usable]

    for copy in loads[: 2 * chains]:
        copy.wait()

    def spread(i):
        return pl.ds(i, BLOCKS, stride=step_count)

    def word_steps(k, _):
        kept_words = [
            bits[chain, pl.ds(k, BLOCKS, stride=words), :] & usable[chain]
            for chain in range(chains)
        ]

        def weigh(j, _):
            i = k * BITS + j
            first = jnp.where(i == 0, 1.0, 0.0)
            last = jnp.where(i == step_count - 1, 1.0, 0.0)
            for h in range(HALVES):
                both = 4.0 * c[h] - 2.0 * c[h] * (at_first * first + at_last * last)
                w_sum = band = None
                for e in range(e_dev):
                    chain = e * HALVES + h
                    iv = ivar[chain, spread(i), :]
                    bit = (kept_words[chain] >> j) & 1
                    w = jnp.where(bit == 1, iv, 0.0)
                    weight[i, chain] = w
                    part = w / (iv + both)
                    w_sum = w if w_sum is None else w_sum + w
                    band = part if band is None else band + part
                sums[0, h, spread(i), :] = w_sum
                sums[1, h, spread(i), :] = band * c[h]
            return 0

        return lax.fori_loop(0, BITS, weigh, 0)

    lax.fori_loop(0, words, word_steps, 0)

    pl.semaphore_wait(barrier, n_fib + 2)

    other_half = pl.ds(pl.multiple_of(partner * half, 8), half)
    my_half = pl.ds(pl.multiple_of(exp * half, 8), half)

    def half_copy(start, count, number):
        return pltpu.make_async_remote_copy(
            sums.at[pl.ds(start, count), :, other_half, :],
            theirs.at[pl.ds(start, count)],
            half_send.at[number],
            half_recv.at[number],
            **to(exp=partner),
        )

    half_a = half_copy(0, 2, 0)
    half_a.start()

    for copy in loads[2 * chains :]:
        copy.wait()

    c_e = [c[h][:e_dev] for h in range(HALVES)]

    def edge_row(ref, h, row):
        return jnp.concatenate(
            [ref[e * HALVES + h, pl.ds(row, 1), :] for e in range(e_dev)], axis=0
        )

    def edge_step(j, state):
        out = []
        for side in range(2):
            for h in range(HALVES):
                d, y = state[side * HALVES + h]
                row = waves - HALO + j if side == 0 else HALO - 1 - j
                iv, px = edge_row(ivar, h, row), edge_row(pix, h, row)
                m = c_e[h] / d
                out.append((iv + 2.0 * c_e[h] - c_e[h] * m, iv * px + m * y))
        return tuple(out)

    start = []
    for side in range(2):
        for h in range(HALVES):
            row = waves - HALO if side == 0 else HALO - 1
            iv, px = edge_row(ivar, h, row), edge_row(pix, h, row)
            start.append((iv + c_e[h], iv * px))
    ends = lax.fori_loop(1, HALO, edge_step, tuple(start))
    for side in range(2):
        for h in range(HALVES):
            for q in range(2):
                edge_out[side, q, pl.ds(h, e_dev, stride=HALVES), :] = ends[side * HALVES + h][q]

    def edge_copy(side):
        return pltpu.make_async_remote_copy(
            edge_out.at[side],
            edge_in.at[side],
            edge_send.at[side],
            edge_recv.at[side],
            **to(wav=wav_right if side == 0 else wav_left),
        )

    edges = [edge_copy(0), edge_copy(1)]
    for copy in edges:
        copy.start()

    def sorted_rows(number, extra):
        mine = [
            sums[number, h, my_half, :] + theirs[number, h, :, :] for h in range(HALVES)
        ]
        x = jnp.concatenate([jnp.concatenate(mine, axis=1), extra], axis=0)
        return exact_dot(sort_ref[...], x, ((1,), (1,)), True)

    def owner_copy(k, src, dst, s_sem, r_sem):
        p = fib_peer(k)
        return pltpu.make_async_remote_copy(
            src.at[pl.ds(pl.multiple_of(p * per, 8), per), :],
            dst.at[pl.ds(pl.multiple_of(fib * per, 8), per), :],
            s_sem.at[k],
            r_sem.at[k],
            **to(fib=p),
        )

    def send_all(src, dst, s_sem, r_sem):
        def one_peer(k, _):
            owner_copy(k, src, dst, s_sem, r_sem).start()
            return 0

        lax.fori_loop(1, n_fib, one_peer, 0)
        mine = pl.ds(pl.multiple_of(fib * per, 8), per)
        dst[mine, :] = src[mine, :]

    def wait_all(src, dst, s_sem, r_sem):
        def one_peer(k, _):
            owner_copy(k, src, dst, s_sem, r_sem).wait()
            return 0

        lax.fori_loop(1, n_fib, one_peer, 0)

    pad = ROWS - half
    blank = jnp.zeros((pad, F_DEV), F32)
    slot_rows = jnp.where(
        lax.broadcasted_iota(jnp.int32, (pad, F_DEV), 0) == SLOT_ROW - half,
        jnp.broadcast_to(slot_f32, (pad, F_DEV)),
        blank,
    )

    half_a.wait()
    send_a[:, pl.ds(0, ROWS)] = sorted_rows(0, slot_rows)
    send_a[:, pl.ds(ROWS, ROWS)] = sorted_rows(1, blank)
    send_all(send_a, got_a, a_send, a_recv)

    def eliminate(i, link, state):
        out = []
        for chain in range(chains):
            h = chain % HALVES
            m, y, s, g, hh = state[chain]
            iv = ivar[chain, spread(i), :]
            b = iv * pix[chain, spread(i), :]
            d = iv + link[h] - c[h] * m
            y = b + m * y
            s = m * s if s is not None else c[h]
            r = 1.0 / d
            m = c[h] * r
            q = s * r
            g = g + q * s
            hh = hh + q * y
            fac_m[i, chain] = m
            fac_y[i, chain] = r * y
            fac_q[i, chain] = q
            out.append((m, y, s, g, hh))
        return tuple(out)

    nothing = jnp.zeros((BLOCKS, LANES), F32)
    state = eliminate(0, link_first, tuple((nothing, nothing, None, nothing, nothing) for _ in range(chains)))
    link_inner = [2.0 * c[h] for h in range(HALVES)]
    last = step_count - 1
    state = lax.fori_loop(1, last, lambda i, st: eliminate(i, link_inner, st), state)

    for chain in range(chains):
        h = chain % HALVES
        m, y, s, g, hh = state[chain]
        iv = ivar[chain, spread(last), :]
        b = iv * pix[chain, spread(last), :]
        rows = pl.ds(chain * BLOCKS, BLOCKS)
        red[0, rows, :] = iv + link_last[h] - c[h] * m
        red[1, rows, :] = b + m * y
        red[2, rows, :] = g
        red[3, rows, :] = hh
        red[4, rows, :] = c[h] * fac_q[last - 1, chain]
        red[5, pl.ds(chain, 1), :] = coupling_ref[pl.ds(h, 1), :]

    for copy in edges:
        copy.wait()

    def across(k, b):
        return red[k, pl.ds(b, chains, stride=BLOCKS), :]

    d_l, y_l = edge_in[0, 0], edge_in[0, 1]
    d_r, y_r = edge_in[1, 0], edge_in[1, 1]
    c_all = red[5, pl.ds(0, chains), :]
    e_b = [across(4, b) for b in range(BLOCKS)]
    d_b, z_b = [], []
    right = c_all / d_r
    for b in range(BLOCKS):
        if b + 1 < BLOCKS:
            g_next, h_next = across(2, b + 1), across(3, b + 1)
        else:
            g_next = jnp.where(wav < n_wav - 1, c_all * right, 0.0)
            h_next = jnp.where(wav < n_wav - 1, y_r * right, 0.0)
        d_b.append(across(0, b) - g_next)
        z_b.append(across(1, b) + h_next)
    r_l = jnp.where(wav > 0, 1.0 / (d_l - across(2, 0)), 0.0)
    p_l = jnp.where(wav > 0, y_l + across(3, 0), 0.0)
    prev_e = e_b[0] * r_l
    d_b[0] = d_b[0] - e_b[0] * prev_e
    z_b[0] = z_b[0] + p_l * prev_e
    inv = []
    for b in range(BLOCKS):
        inv.append(1.0 / d_b[b])
        if b + 1 < BLOCKS:
            prev_e = e_b[b + 1] * inv[b]
            d_b[b + 1] = d_b[b + 1] - e_b[b + 1] * prev_e
            z_b[b + 1] = z_b[b + 1] + z_b[b] * prev_e
    x = None
    for b in reversed(range(BLOCKS)):
        x = inv[b] * (z_b[b] if x is None else z_b[b] + e_b[b + 1] * x)
        far[0, pl.ds(b, chains, stride=BLOCKS), :] = x
        if b + 1 < BLOCKS:
            far[1, pl.ds(b + 1, chains, stride=BLOCKS), :] = x
    far[1, pl.ds(0, chains, stride=BLOCKS), :] = r_l * (p_l + e_b[0] * x)

    def flux_at(i, xs):
        for h in range(HALVES):
            total = None
            for e in range(e_dev):
                chain = e * HALVES + h
                part = weight[i, chain] * xs[chain]
                total = part if total is None else total + part
            sums[2, h, spread(i), :] = total

    xs = [far[0, pl.ds(chain * BLOCKS, BLOCKS), :] for chain in range(chains)]
    lefts = [far[1, pl.ds(chain * BLOCKS, BLOCKS), :] for chain in range(chains)]
    flux_at(last, xs)

    def substitute(k, xs):
        i = last - 1 - k
        xs = tuple(
            fac_y[i, chain] + fac_q[i, chain] * lefts[chain] + fac_m[i, chain] * xs[chain]
            for chain in range(chains)
        )
        flux_at(i, xs)
        return xs

    lax.fori_loop(0, last, substitute, tuple(xs))

    half_b = half_copy(2, 1, 1)
    half_b.start()
    half_b.wait()
    send_b[...] = sorted_rows(2, blank)
    send_all(send_b, got_b, b_send, b_recv)
    wait_all(send_a, got_a, a_send, a_recv)
    wait_all(send_b, got_b, b_send, b_recv)


def finish_kernel(n_wav, a_ref, b_ref, flux_ref, ivar_ref, res_ref):
    wav, exp = lax.axis_index("wav"), lax.axis_index("exp")
    half = flux_ref.shape[0]
    slot = a_ref[:, pl.ds(SLOT_ROW, 1)]
    lane = lax.broadcasted_iota(jnp.int32, (F_DEV, F_DEV), 1).astype(F32)
    one, zero = jnp.ones((), F32), jnp.zeros((), F32)
    place = jnp.where(slot == lane, one, zero).astype(BF16)

    def placed(x):
        return exact_dot(place, x.T, ((1,), (0,)), False)[:half]

    weight_sum = placed(a_ref[:, pl.ds(0, ROWS)])
    band = placed(a_ref[:, pl.ds(ROWS, ROWS)])
    flux_sum = placed(b_ref[...])
    row = lax.broadcasted_iota(jnp.int32, (half, F_DEV), 0)
    first = (row == 0) & (wav == 0) & (exp == 0)
    last = (row == half - 1) & (wav == n_wav - 1) & (exp == 1)
    lower = jnp.where(first, 0.0, band)
    upper = jnp.where(last, 0.0, band)
    divisor = jnp.maximum(weight_sum, 1.0)
    flux_ref[...] = flux_sum / divisor
    ivar_ref[...] = weight_sum
    res_ref[0] = lower / divisor
    res_ref[1] = (weight_sum - lower - upper) / divisor
    res_ref[2] = upper / divisor


def per_device(n_fib, n_wav, pixels, pixel_ivar, clip_bits, coupling, counts, good_flags, owner_slot):
    e_dev, waves, _ = pixels.shape
    n_words = clip_bits.shape[1]
    chains = e_dev * HALVES
    steps = waves // BLOCKS
    half = waves // 2
    vmem = pl.BlockSpec(memory_space=pltpu.VMEM)
    hbm = pl.BlockSpec(memory_space=pl.ANY)
    dma = pltpu.SemaphoreType.DMA
    got_a, got_b = pl.pallas_call(
        functools.partial(exchange_kernel, n_fib, n_wav),
        out_shape=(
            jax.ShapeDtypeStruct((F_DEV, 2 * ROWS), F32),
            jax.ShapeDtypeStruct((F_DEV, ROWS), F32),
        ),
        in_specs=[hbm] * 3 + [vmem] * 4,
        out_specs=(vmem, vmem),
        scratch_shapes=[
            pltpu.VMEM((chains, waves, LANES), F32),
            pltpu.VMEM((chains, waves, LANES), F32),
            pltpu.VMEM((chains, n_words, LANES), jnp.int32),
            pltpu.VMEM((steps, chains, BLOCKS, LANES), F32),
            pltpu.VMEM((steps, chains, BLOCKS, LANES), F32),
            pltpu.VMEM((steps, chains, BLOCKS, LANES), F32),
            pltpu.VMEM((steps, chains, BLOCKS, LANES), F32),
            pltpu.VMEM((3, HALVES, waves, LANES), F32),
            pltpu.VMEM((3, HALVES, half, LANES), F32),
            pltpu.VMEM((F_DEV, 2 * ROWS), F32),
            pltpu.VMEM((F_DEV, ROWS), F32),
            pltpu.VMEM((F_DEV, F_DEV), BF16),
            pltpu.VMEM((2, 2, chains, LANES), F32),
            pltpu.VMEM((2, 2, chains, LANES), F32),
            pltpu.VMEM((6, chains * BLOCKS, LANES), F32),
            pltpu.VMEM((2, chains * BLOCKS, LANES), F32),
            dma((3, chains)),
            dma((2,)),
            dma((2,)),
            dma((2,)),
            dma((2,)),
            dma((n_fib,)),
            dma((n_fib,)),
            dma((n_fib,)),
            dma((n_fib,)),
        ],
        compiler_params=pltpu.CompilerParams(collective_id=0, has_side_effects=True),
        name="exchange",
    )(
        pixels,
        pixel_ivar,
        clip_bits,
        coupling.reshape(HALVES, LANES),
        counts.reshape(HALVES, LANES),
        good_flags,
        owner_slot.reshape(-1, LANES),
    )
    return pl.pallas_call(
        functools.partial(finish_kernel, n_wav),
        out_shape=(
            jax.ShapeDtypeStruct((half, F_DEV), F32),
            jax.ShapeDtypeStruct((half, F_DEV), F32),
            jax.ShapeDtypeStruct((3, half, F_DEV), F32),
        ),
        in_specs=[vmem, vmem],
        out_specs=(vmem, vmem, vmem),
        name="finish",
    )(got_a, got_b)


def solution(mesh):
    return jax.shard_map(
        functools.partial(per_device, mesh.shape["fib"], mesh.shape["wav"]),
        mesh=mesh,
        in_specs=(
            P("exp", "wav", "fib"),
            P("exp", "wav", "fib"),
            P("exp", "wav", "fib"),
            P("fib"),
            P("fib"),
            P("exp", "fib"),
            P(),
        ),
        out_specs=(
            P(("wav", "exp"), "fib"),
            P(("wav", "exp"), "fib"),
            P(None, ("wav", "exp"), "fib"),
        ),
        check_vma=False,
    )
```

profile of v0, /device:TPU:1, one launch (start us, length us, event | category | flops | bytes accessed | tf_op | source)
XLA Modules:
  0.0 38.5 jit_solution(14068918219112091625)
XLA Ops:
  0.6 35.2 %exchange.1 = (f32[256,512]{1,0:T(8,128)}, f32[256,256]{1,0:T(8,128)}) custom-call(f32[4,480,256]{2,1,0:T(8,128)} %pix_hbm.1, f32[4,480,256]{2,1,0:T(8,128)} %ivar_hbm.1, s32[4,32,256]{2,1,0:T(8,128)} %bits_hbm.1, f32[2,128]{1,0:T(2,128)} %bitcast.4, s32[2,128]{1,0:T(2,128)} %bitcast.5, s32[4,256]{1,0:T(4,128)} %good_ref.1, s32[64,128]{1,0:T(8,128)} %bitcast.3), custom_call_target="tpu_custom_call" | custom-call | tf_op jit(solution)/shard_map/exchange/pallas_call | solution.py:452
  35.9 2.7 %finish.1 = (f32[240,256]{1,0:T(8,128)}, f32[240,256]{1,0:T(8,128)}, f32[3,240,256]{2,1,0:T(8,128)}) custom-call(f32[256,512]{1,0:T(8,128)} %get-tuple-element.5.a_ref, f32[256,256]{1,0:T(8,128)} %get-tuple-element.6.b_ref), custom_call_target="tpu_custom_call" | custom-call | tf_op jit(solution)/shard_map/finish/pallas_call | solution.py:498
where the time goes:
time: 38.7 us; the launch traced here: 38.5 us
  Pallas kernels  37.9 us (98%)
  between operations  0.64 us (2%)
    pallas_call x1, Pallas kernels, per_device(): pl.pallas_call(functools.partial(exchange_kernel, n_fib, n_wav), out_shap...  35.2 us
    pallas_call x1, Pallas kernels, per_device(): pl.pallas_call(functools.partial(finish_kernel, n_wav), out_shape=(jax.Sh...  2.68 us

commit v1 on v0

--- a/solution.py
+++ b/solution.py
@@ -15,6 +15,7 @@
 F_DEV = LANES * HALVES
 ROWS = 256
 SLOT_ROW = 240
+RING = 8
 
 F32 = jnp.float32
 BF16 = jnp.bfloat16
@@ -35,6 +36,21 @@
         part = lax.dot_general(*pair, (dims, ((), ())), preferred_element_type=F32)
         total = part if total is None else total + part
     return total
+
+
+def offsets(n_fib):
+    n_z = RING if n_fib % RING == 0 else n_fib
+    n_y = n_fib // n_z
+
+    def hops(o):
+        return min(o[0], n_y - o[0]) + min(o[1], n_z - o[1])
+
+    others = [(dy, dz) for dy in range(n_y) for dz in range(n_z) if dy or dz]
+    return n_y, n_z, sorted(others, key=lambda o: -hops(o))
+
+
+def placed_rows(place, x, count):
+    return exact_dot(place, x.T, ((1,), (0,)), False)[:count]
 
 
 def exchange_kernel(
@@ -47,8 +63,10 @@
     counts_ref,
     good_ref,
     slots_ref,
-    got_a,
-    got_b,
+    place_ref,
+    ivar_out,
+    res_out,
+    got_f,
     pix,
     ivar,
     bits,
@@ -58,8 +76,9 @@
     fac_q,
     sums,
     theirs,
-    send_a,
-    send_b,
+    send,
+    got_w,
+    got_t,
     sort_ref,
     edge_out,
     edge_in,
@@ -70,10 +89,8 @@
     edge_recv,
     half_send,
     half_recv,
-    a_send,
-    a_recv,
-    b_send,
-    b_recv,
+    own_send,
+    own_recv,
 ):
     fib, wav, exp = lax.axis_index("fib"), lax.axis_index("wav"), lax.axis_index("exp")
     e_dev = good_ref.shape[0]
@@ -84,6 +101,28 @@
     half = waves // 2
     per = F_DEV // n_fib
 
+    def to(**where):
+        return {"device_id": where, "device_id_type": pl.DeviceIdType.MESH}
+
+    n_y, n_z, others = offsets(n_fib)
+    fib_y, fib_z = fib // n_z, lax.rem(fib, n_z)
+
+    def fib_peer(k):
+        dy, dz = others[k]
+        return lax.rem(fib_y + dy, n_y) * n_z + lax.rem(fib_z + dz, n_z)
+
+    wav_right = lax.rem(wav + 1, n_wav)
+    wav_left = lax.rem(wav + n_wav - 1, n_wav)
+    partner = 1 - exp
+
+    barrier = pltpu.get_barrier_semaphore()
+
+    for k in range(n_fib - 1):
+        pl.semaphore_signal(barrier, inc=1, **to(fib=fib_peer(k)))
+    pl.semaphore_signal(barrier, inc=1, **to(exp=partner))
+    pl.semaphore_signal(barrier, inc=1, **to(wav=wav_right))
+    pl.semaphore_signal(barrier, inc=1, **to(wav=wav_left))
+
     loads = []
 
     def load(src, dst, rows, number):
@@ -98,27 +137,6 @@
     load(bits_hbm, bits, None, 0)
     load(ivar_hbm, ivar, None, 1)
     load(pix_hbm, pix, None, 2)
-
-    def to(**where):
-        return {"device_id": where, "device_id_type": pl.DeviceIdType.MESH}
-
-    def fib_peer(k):
-        return lax.rem(fib + k, n_fib)
-
-    wav_right = lax.rem(wav + 1, n_wav)
-    wav_left = lax.rem(wav + n_wav - 1, n_wav)
-    partner = 1 - exp
-
-    barrier = pltpu.get_barrier_semaphore()
-
-    def greet(k, _):
-        pl.semaphore_signal(barrier, inc=1, **to(fib=fib_peer(k)))
-        return 0
-
-    pl.semaphore_signal(barrier, inc=1, **to(exp=partner))
-    pl.semaphore_signal(barrier, inc=1, **to(wav=wav_right))
-    pl.semaphore_signal(barrier, inc=1, **to(wav=wav_left))
-    lax.fori_loop(1, n_fib, greet, 0)
 
     slot_row = jnp.concatenate(
         [slots_ref[pl.ds(fib * HALVES + h, 1), :] for h in range(HALVES)], axis=1
@@ -169,22 +187,15 @@
 
         def weigh(j, _):
             i = k * BITS + j
-            first = jnp.where(i == 0, 1.0, 0.0)
-            last = jnp.where(i == step_count - 1, 1.0, 0.0)
             for h in range(HALVES):
-                both = 4.0 * c[h] - 2.0 * c[h] * (at_first * first + at_last * last)
-                w_sum = band = None
+                w_sum = None
                 for e in range(e_dev):
                     chain = e * HALVES + h
-                    iv = ivar[chain, spread(i), :]
                     bit = (kept_words[chain] >> j) & 1
-                    w = jnp.where(bit == 1, iv, 0.0)
+                    w = jnp.where(bit == 1, ivar[chain, spread(i), :], 0.0)
                     weight[i, chain] = w
-                    part = w / (iv + both)
                     w_sum = w if w_sum is None else w_sum + w
-                    band = part if band is None else band + part
                 sums[0, h, spread(i), :] = w_sum
-                sums[1, h, spread(i), :] = band * c[h]
             return 0
 
         return lax.fori_loop(0, BITS, weigh, 0)
@@ -196,17 +207,74 @@
     other_half = pl.ds(pl.multiple_of(partner * half, 8), half)
     my_half = pl.ds(pl.multiple_of(exp * half, 8), half)
 
-    def half_copy(start, count, number):
+    def half_copy(number):
         return pltpu.make_async_remote_copy(
-            sums.at[pl.ds(start, count), :, other_half, :],
-            theirs.at[pl.ds(start, count)],
+            sums.at[number, :, other_half, :],
+            theirs.at[number],
             half_send.at[number],
             half_recv.at[number],
             **to(exp=partner),
         )
 
-    half_a = half_copy(0, 2, 0)
-    half_a.start()
+    half_w = half_copy(0)
+    half_w.start()
+
+    def band_step(i, _):
+        first = jnp.where(i == 0, 1.0, 0.0)
+        last = jnp.where(i == step_count - 1, 1.0, 0.0)
+        for h in range(HALVES):
+            both = 4.0 * c[h] - 2.0 * c[h] * (at_first * first + at_last * last)
+            band = None
+            for e in range(e_dev):
+                chain = e * HALVES + h
+                part = weight[i, chain] / (ivar[chain, spread(i), :] + both)
+                band = part if band is None else band + part
+            sums[1, h, spread(i), :] = band * c[h]
+        return 0
+
+    lax.fori_loop(0, step_count, band_step, 0)
+    half_t = half_copy(1)
+    half_t.start()
+
+    def sorted_rows(number, extra):
+        mine = [
+            sums[number, h, my_half, :] + theirs[number, h, :, :] for h in range(HALVES)
+        ]
+        x = jnp.concatenate([jnp.concatenate(mine, axis=1), extra], axis=0)
+        return exact_dot(sort_ref[...], x, ((1,), (1,)), True)
+
+    got = (got_w, got_t, got_f)
+    mine = pl.ds(pl.multiple_of(fib * per, 8), per)
+
+    def owner_copy(number, k):
+        p = fib_peer(k)
+        return pltpu.make_async_remote_copy(
+            send.at[number, pl.ds(pl.multiple_of(p * per, 8), per), :],
+            got[number].at[mine, :],
+            own_send.at[number, k],
+            own_recv.at[number, k],
+            **to(fib=p),
+        )
+
+    def send_all(number, extra):
+        send[number] = sorted_rows(number, extra)
+        for k in range(n_fib - 1):
+            owner_copy(number, k).start()
+        got[number][mine, :] = send[number, mine, :]
+
+    def wait_all(number):
+        for k in range(n_fib - 1):
+            owner_copy(number, k).wait()
+
+    pad = ROWS - half
+    blank = jnp.zeros((pad, F_DEV), F32)
+    slot_rows = jnp.where(
+        lax.broadcasted_iota(jnp.int32, (pad, F_DEV), 0) == SLOT_ROW - half,
+        jnp.broadcast_to(slot_f32, (pad, F_DEV)),
+        blank,
+    )
+    half_w.wait()
+    send_all(0, slot_rows)
 
     for copy in loads[2 * chains :]:
         copy.wait()
@@ -254,51 +322,8 @@
     for copy in edges:
         copy.start()
 
-    def sorted_rows(number, extra):
-        mine = [
-            sums[number, h, my_half, :] + theirs[number, h, :, :] for h in range(HALVES)
-        ]
-        x = jnp.concatenate([jnp.concatenate(mine, axis=1), extra], axis=0)
-        return exact_dot(sort_ref[...], x, ((1,), (1,)), True)
-
-    def owner_copy(k, src, dst, s_sem, r_sem):
-        p = fib_peer(k)
-        return pltpu.make_async_remote_copy(
-            src.at[pl.ds(pl.multiple_of(p * per, 8), per), :],
-            dst.at[pl.ds(pl.multiple_of(fib * per, 8), per), :],
-            s_sem.at[k],
-            r_sem.at[k],
-            **to(fib=p),
-        )
-
-    def send_all(src, dst, s_sem, r_sem):
-        def one_peer(k, _):
-            owner_copy(k, src, dst, s_sem, r_sem).start()
-            return 0
-
-        lax.fori_loop(1, n_fib, one_peer, 0)
-        mine = pl.ds(pl.multiple_of(fib * per, 8), per)
-        dst[mine, :] = src[mine, :]
-
-    def wait_all(src, dst, s_sem, r_sem):
-        def one_peer(k, _):
-            owner_copy(k, src, dst, s_sem, r_sem).wait()
-            return 0
-
-        lax.fori_loop(1, n_fib, one_peer, 0)
-
-    pad = ROWS - half
-    blank = jnp.zeros((pad, F_DEV), F32)
-    slot_rows = jnp.where(
-        lax.broadcasted_iota(jnp.int32, (pad, F_DEV), 0) == SLOT_ROW - half,
-        jnp.broadcast_to(slot_f32, (pad, F_DEV)),
-        blank,
-    )
-
-    half_a.wait()
-    send_a[:, pl.ds(0, ROWS)] = sorted_rows(0, slot_rows)
-    send_a[:, pl.ds(ROWS, ROWS)] = sorted_rows(1, blank)
-    send_all(send_a, got_a, a_send, a_recv)
+    half_t.wait()
+    send_all(1, blank)
 
     def eliminate(i, link, state):
         out = []
@@ -404,40 +429,43 @@
 
     lax.fori_loop(0, last, substitute, tuple(xs))
 
-    half_b = half_copy(2, 1, 1)
-    half_b.start()
-    half_b.wait()
-    send_b[...] = sorted_rows(2, blank)
-    send_all(send_b, got_b, b_send, b_recv)
-    wait_all(send_a, got_a, a_send, a_recv)
-    wait_all(send_b, got_b, b_send, b_recv)
-
-
-def finish_kernel(n_wav, a_ref, b_ref, flux_ref, ivar_ref, res_ref):
-    wav, exp = lax.axis_index("wav"), lax.axis_index("exp")
-    half = flux_ref.shape[0]
-    slot = a_ref[:, pl.ds(SLOT_ROW, 1)]
+    half_f = half_copy(2)
+    half_f.start()
+    half_f.wait()
+    send_all(2, blank)
+
+    wait_all(0)
+    slot = got_w[:, pl.ds(SLOT_ROW, 1)]
     lane = lax.broadcasted_iota(jnp.int32, (F_DEV, F_DEV), 1).astype(F32)
-    one, zero = jnp.ones((), F32), jnp.zeros((), F32)
-    place = jnp.where(slot == lane, one, zero).astype(BF16)
-
-    def placed(x):
-        return exact_dot(place, x.T, ((1,), (0,)), False)[:half]
-
-    weight_sum = placed(a_ref[:, pl.ds(0, ROWS)])
-    band = placed(a_ref[:, pl.ds(ROWS, ROWS)])
-    flux_sum = placed(b_ref[...])
+    place_ref[...] = jnp.where(slot == lane, one, zero).astype(BF16)
+    place = place_ref[...]
+    ivar_out[...] = placed_rows(place, got_w[...], half)
+    wait_all(1)
+    band = placed_rows(place, got_t[...], half)
+    weight_sum = ivar_out[...]
     row = lax.broadcasted_iota(jnp.int32, (half, F_DEV), 0)
-    first = (row == 0) & (wav == 0) & (exp == 0)
-    last = (row == half - 1) & (wav == n_wav - 1) & (exp == 1)
-    lower = jnp.where(first, 0.0, band)
-    upper = jnp.where(last, 0.0, band)
+    lower = jnp.where((row == 0) & (wav == 0) & (exp == 0), 0.0, band)
+    upper = jnp.where((row == half - 1) & (wav == n_wav - 1) & (exp == 1), 0.0, band)
     divisor = jnp.maximum(weight_sum, 1.0)
-    flux_ref[...] = flux_sum / divisor
-    ivar_ref[...] = weight_sum
-    res_ref[0] = lower / divisor
-    res_ref[1] = (weight_sum - lower - upper) / divisor
-    res_ref[2] = upper / divisor
+    res_out[0] = lower / divisor
+    res_out[1] = (weight_sum - lower - upper) / divisor
+    res_out[2] = upper / divisor
+    wait_all(2)
+
+
+def finish_kernel(place_ref, ivar_ref, res_ref, got_ref, flux_hbm, ivar_hbm, res_hbm, flux, sems):
+    half = ivar_ref.shape[0]
+    copies = [
+        pltpu.make_async_copy(ivar_ref, ivar_hbm, sems.at[0]),
+        pltpu.make_async_copy(res_ref, res_hbm, sems.at[1]),
+        pltpu.make_async_copy(flux, flux_hbm, sems.at[2]),
+    ]
+    copies[0].start()
+    copies[1].start()
+    flux[...] = placed_rows(place_ref[...], got_ref[...], half) / jnp.maximum(ivar_ref[...], 1.0)
+    copies[2].start()
+    for copy in copies:
+        copy.wait()
 
 
 def per_device(n_fib, n_wav, pixels, pixel_ivar, clip_bits, coupling, counts, good_flags, owner_slot):
@@ -447,16 +475,19 @@
     steps = waves // BLOCKS
     half = waves // 2
     vmem = pl.BlockSpec(memory_space=pltpu.VMEM)
-    hbm = pl.BlockSpec(memory_space=pl.ANY)
+    hbm = pl.BlockSpec(memory_space=pltpu.HBM)
     dma = pltpu.SemaphoreType.DMA
-    got_a, got_b = pl.pallas_call(
+    limit = 24 * 2**20
+    parts = pl.pallas_call(
         functools.partial(exchange_kernel, n_fib, n_wav),
         out_shape=(
-            jax.ShapeDtypeStruct((F_DEV, 2 * ROWS), F32),
+            jax.ShapeDtypeStruct((F_DEV, F_DEV), BF16),
+            jax.ShapeDtypeStruct((half, F_DEV), F32),
+            jax.ShapeDtypeStruct((3, half, F_DEV), F32),
             jax.ShapeDtypeStruct((F_DEV, ROWS), F32),
         ),
         in_specs=[hbm] * 3 + [vmem] * 4,
-        out_specs=(vmem, vmem),
+        out_specs=(vmem,) * 4,
         scratch_shapes=[
             pltpu.VMEM((chains, waves, LANES), F32),
             pltpu.VMEM((chains, waves, LANES), F32),
@@ -467,7 +498,8 @@
             pltpu.VMEM((steps, chains, BLOCKS, LANES), F32),
             pltpu.VMEM((3, HALVES, waves, LANES), F32),
             pltpu.VMEM((3, HALVES, half, LANES), F32),
-            pltpu.VMEM((F_DEV, 2 * ROWS), F32),
+            pltpu.VMEM((3, F_DEV, ROWS), F32),
+            pltpu.VMEM((F_DEV, ROWS), F32),
             pltpu.VMEM((F_DEV, ROWS), F32),
             pltpu.VMEM((F_DEV, F_DEV), BF16),
             pltpu.VMEM((2, 2, chains, LANES), F32),
@@ -477,35 +509,42 @@
             dma((3, chains)),
             dma((2,)),
             dma((2,)),
-            dma((2,)),
-            dma((2,)),
-            dma((n_fib,)),
-            dma((n_fib,)),
-            dma((n_fib,)),
-            dma((n_fib,)),
+            dma((3,)),
+            dma((3,)),
+            dma((3, n_fib - 1)),
+            dma((3, n_fib - 1)),
         ],
-        compiler_params=pltpu.CompilerParams(collective_id=0, has_side_effects=True),
+        compiler_params=pltpu.CompilerParams(
+            collective_id=0, has_side_effects=True, vmem_limit_bytes=limit
+        ),
         name="exchange",
     )(
-        pixels,
-        pixel_ivar,
-        clip_bits,
-        coupling.reshape(HALVES, LANES),
-        counts.reshape(HALVES, LANES),
-        good_flags,
-        owner_slot.reshape(-1, LANES),
+        *(
+            pltpu.with_memory_space_constraint(x, pltpu.HBM)
+            for x in (
+                pixels,
+                pixel_ivar,
+                clip_bits,
+                coupling.reshape(HALVES, LANES),
+                counts.reshape(HALVES, LANES),
+                good_flags,
+                owner_slot.reshape(-1, LANES),
+            )
+        )
     )
     return pl.pallas_call(
-        functools.partial(finish_kernel, n_wav),
+        finish_kernel,
         out_shape=(
             jax.ShapeDtypeStruct((half, F_DEV), F32),
             jax.ShapeDtypeStruct((half, F_DEV), F32),
             jax.ShapeDtypeStruct((3, half, F_DEV), F32),
         ),
-        in_specs=[vmem, vmem],
-        out_specs=(vmem, vmem, vmem),
+        in_specs=[vmem] * 4,
+        out_specs=(hbm,) * 3,
+        scratch_shapes=[pltpu.VMEM((half, F_DEV), F32), dma((3,))],
+        compiler_params=pltpu.CompilerParams(vmem_limit_bytes=8 * 2**20),
         name="finish",
-    )(got_a, got_b)
+    )(*parts)
 
 
 def solution(mesh):

time: 38.7 us -> 35.7 us (0.922)
  Pallas kernels: 37.9 us -> 34.9 us
    pallas_call x1, Pallas kernels: 2.68 us -> 1.05 us  [per_device(): pl.pallas_call(finish_kernel, out_shape=(jax.ShapeDtypeStruct((half, F_DE...]
    pallas_call x1, Pallas kernels: 35.2 us -> 33.9 us  [per_device(): pl.pallas_call(functools.partial(exchange_kernel, n_fib, n_wav), out_shap...]
where the time goes in v1:
time: 35.7 us; the launch traced here: 35.6 us
  Pallas kernels  34.9 us (98%)
  between operations  0.64 us (2%)
    pallas_call x1, Pallas kernels, per_device(): pl.pallas_call(functools.partial(exchange_kernel, n_fib, n_wav), out_shap...  33.9 us
    pallas_call x1, Pallas kernels, per_device(): pl.pallas_call(finish_kernel, out_shape=(jax.ShapeDtypeStruct((half, F_DE...  1.05 us

profile of v1, /device:TPU:1, one launch (start us, length us, event | category | flops | bytes accessed | tf_op | source)
XLA Modules:
  0.0 35.6 jit_solution(8314796874646279331)
XLA Ops:
  0.6 33.9 %exchange.1 = (bf16[256,256]{1,0:T(8,128)(2,1)S(1)}, f32[240,256]{1,0:T(8,128)S(1)}, f32[3,240,256]{2,1,0:T(8,128)S(1)}, f32[256,256]{1,0:T(8,128)S(1)}) custom-call(f32[4,480,256]{2,1,0:T(8,128)} %pix_hbm.1, f32[4,480,256]{2,1,0:T(8,128)} %ivar_hbm.1, s32[4,32,256]{2,1,0:T(8,128)} %bits_hbm.1, f32[2,128]{1,0:T(2,128)} %bitcast.4, s32[2,128]{1,0:T(2,128)} %bitcast.5, ...), custom_call_target="tpu_custom_call" | custom-call | tf_op jit(solution)/shard_map/exchange/pallas_call | solution.py:481
  34.5 1.0 %finish.1 = (f32[240,256]{1,0:T(8,128)}, f32[240,256]{1,0:T(8,128)}, f32[3,240,256]{2,1,0:T(8,128)}) custom-call(bf16[256,256]{1,0:T(8,128)(2,1)S(1)} %get-tuple-element.7.place_ref, f32[240,256]{1,0:T(8,128)S(1)} %get-tuple-element.8.ivar_ref, f32[3,240,256]{2,1,0:T(8,128)S(1)} %get-tuple-element.9.res_ref, f32[256,256]{1,0:T(8,128)S(1)} %get-tuple-element.10.got_ref), custom_call_target="tpu_custom_call" | custom-call | tf_op jit(solution)/shard_map/finish/pallas_call | solution.py:535

commit v2 on v1

--- a/solution.py
+++ b/solution.py
@@ -13,7 +13,8 @@
 LANES = 128
 HALVES = 2
 F_DEV = LANES * HALVES
-ROWS = 256
+TILES = 2
+ROWS = LANES * TILES
 SLOT_ROW = 240
 RING = 8
 
@@ -49,8 +50,9 @@
     return n_y, n_z, sorted(others, key=lambda o: -hops(o))
 
 
-def placed_rows(place, x, count):
-    return exact_dot(place, x.T, ((1,), (0,)), False)[:count]
+def placed_rows(place, got_ref, count):
+    x = jnp.concatenate([got_ref[tile].T for tile in range(TILES)], axis=0)
+    return exact_dot(place, x, ((1,), (0,)), False)[:count]
 
 
 def exchange_kernel(
@@ -59,14 +61,18 @@
     pix_hbm,
     ivar_hbm,
     bits_hbm,
+    coupling_hbm,
+    counts_hbm,
+    good_hbm,
+    slots_hbm,
+    place_ref,
+    ivar_out,
+    res_out,
+    got_f,
     coupling_ref,
     counts_ref,
     good_ref,
     slots_ref,
-    place_ref,
-    ivar_out,
-    res_out,
-    got_f,
     pix,
     ivar,
     bits,
@@ -75,7 +81,8 @@
     fac_y,
     fac_q,
     sums,
-    theirs,
+    give,
+    take,
     send,
     got_w,
     got_t,
@@ -84,6 +91,7 @@
     edge_in,
     red,
     far,
+    small_sem,
     load_sem,
     edge_send,
     edge_recv,
@@ -111,6 +119,10 @@
         dy, dz = others[k]
         return lax.rem(fib_y + dy, n_y) * n_z + lax.rem(fib_z + dz, n_z)
 
+    def fib_from(k):
+        dy, dz = others[k]
+        return lax.rem(fib_y + n_y - dy, n_y) * n_z + lax.rem(fib_z + n_z - dz, n_z)
+
     wav_right = lax.rem(wav + 1, n_wav)
     wav_left = lax.rem(wav + n_wav - 1, n_wav)
     partner = 1 - exp
@@ -123,6 +135,19 @@
     pl.semaphore_signal(barrier, inc=1, **to(wav=wav_right))
     pl.semaphore_signal(barrier, inc=1, **to(wav=wav_left))
 
+    small = [
+        pltpu.make_async_copy(src, dst, small_sem.at[number])
+        for number, (src, dst) in enumerate(
+            (
+                (slots_hbm, slots_ref),
+                (coupling_hbm, coupling_ref),
+                (counts_hbm, counts_ref),
+                (good_hbm, good_ref),
+            )
+        )
+    ]
+    for copy in small:
+        copy.start()
     loads = []
 
     def load(src, dst, rows, number):
@@ -137,6 +162,9 @@
     load(bits_hbm, bits, None, 0)
     load(ivar_hbm, ivar, None, 1)
     load(pix_hbm, pix, None, 2)
+
+    for copy in small:
+        copy.wait()
 
     slot_row = jnp.concatenate(
         [slots_ref[pl.ds(fib * HALVES + h, 1), :] for h in range(HALVES)], axis=1
@@ -202,22 +230,66 @@
 
     lax.fori_loop(0, words, word_steps, 0)
 
-    pl.semaphore_wait(barrier, n_fib + 2)
-
+    pad = ROWS - half
+    blank = jnp.zeros((pad, F_DEV), F32)
+    slot_rows = jnp.where(
+        lax.broadcasted_iota(jnp.int32, (pad, F_DEV), 0) == SLOT_ROW - half,
+        jnp.broadcast_to(slot_f32, (pad, F_DEV)),
+        blank,
+    )
+    my_half = pl.ds(pl.multiple_of(exp * half, 8), half)
     other_half = pl.ds(pl.multiple_of(partner * half, 8), half)
-    my_half = pl.ds(pl.multiple_of(exp * half, 8), half)
-
-    def half_copy(number):
+
+    def sort(number, rows, extra, dst):
+        x = jnp.concatenate([sums[number, h, rows, :] for h in range(HALVES)], axis=1)
+        x = jnp.concatenate([x, extra], axis=0)
+        x = exact_dot(sort_ref[...], x, ((1,), (1,)), True)
+        for tile in range(TILES):
+            dst[number, tile] = x[:, tile * LANES : (tile + 1) * LANES]
+
+    def give_copy(number, tile):
         return pltpu.make_async_remote_copy(
-            sums.at[number, :, other_half, :],
-            theirs.at[number],
-            half_send.at[number],
-            half_recv.at[number],
+            give.at[number, tile],
+            take.at[number, tile],
+            half_send.at[number, tile],
+            half_recv.at[number, tile],
             **to(exp=partner),
         )
 
-    half_w = half_copy(0)
-    half_w.start()
+    def give_all(number):
+        for tile in range(TILES):
+            give_copy(number, tile).start()
+        sort(number, my_half, slot_rows if number == 0 else blank, send)
+
+    got = (got_w, got_t, got_f)
+    mine = pl.ds(pl.multiple_of(fib * per, 8), per)
+
+    def owner_copy(number, k, source):
+        p = pl.ds(pl.multiple_of(fib_peer(k) * per, 8), per)
+        q = pl.ds(pl.multiple_of(source * per, 8), per)
+        return pltpu.make_async_remote_copy(
+            send.at[number, :, p, :],
+            got[number].at[:, q, :],
+            own_send.at[number, k],
+            own_recv.at[number, k],
+            **to(fib=fib_peer(k)),
+        )
+
+    def send_all(number):
+        for tile in range(TILES):
+            give_copy(number, tile).wait()
+            send[number, tile] = send[number, tile] + take[number, tile]
+            got[number][tile, mine, :] = send[number, tile, mine, :]
+        for k in range(n_fib - 1):
+            owner_copy(number, k, fib).start()
+
+    def wait_all(number):
+        for k in range(n_fib - 1):
+            owner_copy(number, k, fib_from(k)).wait()
+
+    sort(0, other_half, blank, give)
+    pl.semaphore_wait(barrier, n_fib + 2)
+    give_all(0)
 
     def band_step(i, _):
         first = jnp.where(i == 0, 1.0, 0.0)
@@ -233,48 +305,9 @@
         return 0
 
     lax.fori_loop(0, step_count, band_step, 0)
-    half_t = half_copy(1)
-    half_t.start()
-
-    def sorted_rows(number, extra):
-        mine = [
-            sums[number, h, my_half, :] + theirs[number, h, :, :] for h in range(HALVES)
-        ]
-        x = jnp.concatenate([jnp.concatenate(mine, axis=1), extra], axis=0)
-        return exact_dot(sort_ref[...], x, ((1,), (1,)), True)
-
-    got = (got_w, got_t, got_f)
-    mine = pl.ds(pl.multiple_of(fib * per, 8), per)
-
-    def owner_copy(number, k):
-        p = fib_peer(k)
-        return pltpu.make_async_remote_copy(
-            send.at[number, pl.ds(pl.multiple_of(p * per, 8), per), :],
-            got[number].at[mine, :],
-            own_send.at[number, k],
-            own_recv.at[number, k],
-            **to(fib=p),
-        )
-
-    def send_all(number, extra):
-        send[number] = sorted_rows(number, extra)
-        for k in range(n_fib - 1):
-            owner_copy(number, k).start()
-        got[number][mine, :] = send[number, mine, :]
-
-    def wait_all(number):
-        for k in range(n_fib - 1):
-            owner_copy(number, k).wait()
-
-    pad = ROWS - half
-    blank = jnp.zeros((pad, F_DEV), F32)
-    slot_rows = jnp.where(
-        lax.broadcasted_iota(jnp.int32, (pad, F_DEV), 0) == SLOT_ROW - half,
-        jnp.broadcast_to(slot_f32, (pad, F_DEV)),
-        blank,
-    )
-    half_w.wait()
-    send_all(0, slot_rows)
+    send_all(0)
+    sort(1, other_half, blank, give)
+    give_all(1)
 
     for copy in loads[2 * chains :]:
         copy.wait()
@@ -321,9 +354,7 @@
     edges = [edge_copy(0), edge_copy(1)]
     for copy in edges:
         copy.start()
-
-    half_t.wait()
-    send_all(1, blank)
+    send_all(1)
 
     def eliminate(i, link, state):
         out = []
@@ -429,19 +460,18 @@
 
     lax.fori_loop(0, last, substitute, tuple(xs))
 
-    half_f = half_copy(2)
-    half_f.start()
-    half_f.wait()
-    send_all(2, blank)
+    sort(2, other_half, blank, give)
+    give_all(2)
+    send_all(2)
 
     wait_all(0)
-    slot = got_w[:, pl.ds(SLOT_ROW, 1)]
+    slot = got_w[SLOT_ROW // LANES, :, pl.ds(SLOT_ROW % LANES, 1)]
     lane = lax.broadcasted_iota(jnp.int32, (F_DEV, F_DEV), 1).astype(F32)
     place_ref[...] = jnp.where(slot == lane, one, zero).astype(BF16)
     place = place_ref[...]
-    ivar_out[...] = placed_rows(place, got_w[...], half)
+    ivar_out[...] = placed_rows(place, got_w, half)
     wait_all(1)
-    band = placed_rows(place, got_t[...], half)
+    band = placed_rows(place, got_t, half)
     weight_sum = ivar_out[...]
     row = lax.broadcasted_iota(jnp.int32, (half, F_DEV), 0)
     lower = jnp.where((row == 0) & (wav == 0) & (exp == 0), 0.0, band)
@@ -462,7 +492,7 @@
     ]
     copies[0].start()
     copies[1].start()
-    flux[...] = placed_rows(place_ref[...], got_ref[...], half) / jnp.maximum(ivar_ref[...], 1.0)
+    flux[...] = placed_rows(place_ref[...], got_ref, half) / jnp.maximum(ivar_ref[...], 1.0)
     copies[2].start()
     for copy in copies:
         copy.wait()
@@ -484,11 +514,15 @@
             jax.ShapeDtypeStruct((F_DEV, F_DEV), BF16),
             jax.ShapeDtypeStruct((half, F_DEV), F32),
             jax.ShapeDtypeStruct((3, half, F_DEV), F32),
-            jax.ShapeDtypeStruct((F_DEV, ROWS), F32),
+            jax.ShapeDtypeStruct((TILES, F_DEV, LANES), F32),
         ),
-        in_specs=[hbm] * 3 + [vmem] * 4,
+        in_specs=[hbm] * 7,
         out_specs=(vmem,) * 4,
         scratch_shapes=[
+            pltpu.VMEM((HALVES, LANES), F32),
+            pltpu.VMEM((HALVES, LANES), jnp.int32),
+            pltpu.VMEM(good_flags.shape, jnp.int32),
+            pltpu.VMEM((owner_slot.shape[0] // LANES, LANES), jnp.int32),
             pltpu.VMEM((chains, waves, LANES), F32),
             pltpu.VMEM((chains, waves, LANES), F32),
             pltpu.VMEM((chains, n_words, LANES), jnp.int32),
@@ -497,20 +531,22 @@
             pltpu.VMEM((steps, chains, BLOCKS, LANES), F32),
             pltpu.VMEM((steps, chains, BLOCKS, LANES), F32),
             pltpu.VMEM((3, HALVES, waves, LANES), F32),
-            pltpu.VMEM((3, HALVES, half, LANES), F32),
-            pltpu.VMEM((3, F_DEV, ROWS), F32),
-            pltpu.VMEM((F_DEV, ROWS), F32),
-            pltpu.VMEM((F_DEV, ROWS), F32),
+            pltpu.VMEM((3, TILES, F_DEV, LANES), F32),
+            pltpu.VMEM((3, TILES, F_DEV, LANES), F32),
+            pltpu.VMEM((3, TILES, F_DEV, LANES), F32),
+            pltpu.VMEM((TILES, F_DEV, LANES), F32),
+            pltpu.VMEM((TILES, F_DEV, LANES), F32),
             pltpu.VMEM((F_DEV, F_DEV), BF16),
             pltpu.VMEM((2, 2, chains, LANES), F32),
             pltpu.VMEM((2, 2, chains, LANES), F32),
             pltpu.VMEM((6, chains * BLOCKS, LANES), F32),
             pltpu.VMEM((2, chains * BLOCKS, LANES), F32),
+            dma((4,)),
             dma((3, chains)),
             dma((2,)),
             dma((2,)),
-            dma((3,)),
-            dma((3,)),
+            dma((3, TILES)),
+            dma((3, TILES)),
             dma((3, n_fib - 1)),
             dma((3, n_fib - 1)),
         ],

time: 35.7 us -> 34.9 us (0.978)
  Pallas kernels: 34.9 us -> 33.9 us
    pallas_call x1, Pallas kernels: 33.9 us -> 32.8 us  [per_device(): pl.pallas_call(functools.partial(exchange_kernel, n_fib, n_wav), out_shap...]
where the time goes in v2:
time: 34.9 us; the launch traced here: 34.5 us
  Pallas kernels  33.9 us (97%)
  between operations  0.64 us (2%)
    pallas_call x1, Pallas kernels, per_device(): pl.pallas_call(functools.partial(exchange_kernel, n_fib, n_wav), out_shap...  32.8 us
    pallas_call x1, Pallas kernels, per_device(): pl.pallas_call(finish_kernel, out_shape=(jax.ShapeDtypeStruct((half, F_DE...  1.05 us

profile of v2, /device:TPU:1, one launch (start us, length us, event | category | flops | bytes accessed | tf_op | source)
XLA Modules:
  0.0 34.5 jit_solution(13419726784572673)
XLA Ops:
  0.6 32.8 %exchange.1 = (bf16[256,256]{1,0:T(8,128)(2,1)S(1)}, f32[240,256]{1,0:T(8,128)S(1)}, f32[3,240,256]{2,1,0:T(8,128)S(1)}, f32[2,256,128]{2,1,0:T(8,128)S(1)}) custom-call(f32[4,480,256]{2,1,0:T(8,128)} %pix_hbm.1, f32[4,480,256]{2,1,0:T(8,128)} %ivar_hbm.1, s32[4,32,256]{2,1,0:T(8,128)} %bits_hbm.1, f32[2,128]{1,0:T(2,128)} %bitcast.4, s32[2,128]{1,0:T(2,128)} %bitcast.5, ...), custom_call_target="tpu_custom_call" | custom-call | tf_op jit(solution)/shard_map/exchange/pallas_call | solution.py:511
  33.5 1.0 %finish.1 = (f32[240,256]{1,0:T(8,128)}, f32[240,256]{1,0:T(8,128)}, f32[3,240,256]{2,1,0:T(8,128)}) custom-call(bf16[256,256]{1,0:T(8,128)(2,1)S(1)} %get-tuple-element.7.place_ref, f32[240,256]{1,0:T(8,128)S(1)} %get-tuple-element.8.ivar_ref, f32[3,240,256]{2,1,0:T(8,128)S(1)} %get-tuple-element.9.res_ref, f32[2,256,128]{2,1,0:T(8,128)S(1)} %get-tuple-element.10.got_ref), custom_call_target="tpu_custom_call" | custom-call | tf_op jit(solution)/shard_map/finish/pallas_call | solution.py:571

commit v3 on v2

--- a/solution.py
+++ b/solution.py
@@ -127,14 +127,6 @@
     wav_left = lax.rem(wav + n_wav - 1, n_wav)
     partner = 1 - exp
 
-    barrier = pltpu.get_barrier_semaphore()
-
-    for k in range(n_fib - 1):
-        pl.semaphore_signal(barrier, inc=1, **to(fib=fib_peer(k)))
-    pl.semaphore_signal(barrier, inc=1, **to(exp=partner))
-    pl.semaphore_signal(barrier, inc=1, **to(wav=wav_right))
-    pl.semaphore_signal(barrier, inc=1, **to(wav=wav_left))
-
     small = [
         pltpu.make_async_copy(src, dst, small_sem.at[number])
         for number, (src, dst) in enumerate(
@@ -161,6 +153,15 @@
 
     load(bits_hbm, bits, None, 0)
     load(ivar_hbm, ivar, None, 1)
+
+    barrier = pltpu.get_barrier_semaphore()
+
+    for k in range(n_fib - 1):
+        pl.semaphore_signal(barrier, inc=1, **to(fib=fib_peer(k)))
+    pl.semaphore_signal(barrier, inc=1, **to(exp=partner))
+    pl.semaphore_signal(barrier, inc=1, **to(wav=wav_right))
+    pl.semaphore_signal(barrier, inc=1, **to(wav=wav_left))
+
     load(pix_hbm, pix, None, 2)
 
     for copy in small:
@@ -226,7 +227,7 @@
                 sums[0, h, spread(i), :] = w_sum
             return 0
 
-        return lax.fori_loop(0, BITS, weigh, 0)
+        return lax.fori_loop(0, BITS, weigh, 0, unroll=5)
 
     lax.fori_loop(0, words, word_steps, 0)
 

time: 34.9 us -> 34.6 us (level)
  no operation moved by 1% of the time
where the time goes in v3:
time: 34.6 us
  Pallas kernels  33.9 us (98%)
  between operations  0.64 us (2%)
    pallas_call x1, Pallas kernels, per_device(): pl.pallas_call(functools.partial(exchange_kernel, n_fib, n_wav), out_shap...  32.9 us
    pallas_call x1, Pallas kernels, per_device(): pl.pallas_call(finish_kernel, out_shape=(jax.ShapeDtypeStruct((half, F_DE...  1.05 us

profile of v3, /device:TPU:1, one launch (start us, length us, event | category | flops | bytes accessed | tf_op | source)
XLA Modules:
  0.0 34.6 jit_solution(2523951017645848159)
XLA Ops:
  0.6 32.9 %exchange.1 = (bf16[256,256]{1,0:T(8,128)(2,1)S(1)}, f32[240,256]{1,0:T(8,128)S(1)}, f32[3,240,256]{2,1,0:T(8,128)S(1)}, f32[2,256,128]{2,1,0:T(8,128)S(1)}) custom-call(f32[4,480,256]{2,1,0:T(8,128)} %pix_hbm.1, f32[4,480,256]{2,1,0:T(8,128)} %ivar_hbm.1, s32[4,32,256]{2,1,0:T(8,128)} %bits_hbm.1, f32[2,128]{1,0:T(2,128)} %bitcast.4, s32[2,128]{1,0:T(2,128)} %bitcast.5, ...), custom_call_target="tpu_custom_call" | custom-call | tf_op jit(solution)/shard_map/exchange/pallas_call | solution.py:512
  33.5 1.0 %finish.1 = (f32[240,256]{1,0:T(8,128)}, f32[240,256]{1,0:T(8,128)}, f32[3,240,256]{2,1,0:T(8,128)}) custom-call(bf16[256,256]{1,0:T(8,128)(2,1)S(1)} %get-tuple-element.7.place_ref, f32[240,256]{1,0:T(8,128)S(1)} %get-tuple-element.8.ivar_ref, f32[3,240,256]{2,1,0:T(8,128)S(1)} %get-tuple-element.9.res_ref, f32[2,256,128]{2,1,0:T(8,128)S(1)} %get-tuple-element.10.got_ref), custom_call_target="tpu_custom_call" | custom-call | tf_op jit(solution)/shard_map/finish/pallas_call | solution.py:572

commit v4 on v3

--- a/solution.py
+++ b/solution.py
@@ -265,6 +265,16 @@
     got = (got_w, got_t, got_f)
     mine = pl.ds(pl.multiple_of(fib * per, 8), per)
 
+    def tile_copy(number, k, tile):
+        p = pl.ds(pl.multiple_of(fib_peer(k) * per, 8), per)
+        return pltpu.make_async_remote_copy(
+            send.at[number, tile, p, :],
+            got[number].at[tile, mine, :],
+            own_send.at[number, k],
+            own_recv.at[number, k],
+            **to(fib=fib_peer(k)),
+        )
+
     def owner_copy(number, k, source):
         p = pl.ds(pl.multiple_of(fib_peer(k) * per, 8), per)
         q = pl.ds(pl.multiple_of(source * per, 8), per)
@@ -281,8 +291,8 @@
             give_copy(number, tile).wait()
             send[number, tile] = send[number, tile] + take[number, tile]
             got[number][tile, mine, :] = send[number, tile, mine, :]
-        for k in range(n_fib - 1):
-            owner_copy(number, k, fib).start()
+            for k in range(n_fib - 1):
+                tile_copy(number, k, tile).start()
 
     def wait_all(number):
         for k in range(n_fib - 1):
@@ -292,6 +302,7 @@
     pl.semaphore_wait(barrier, n_fib + 2)
     give_all(0)
 
+    send_all(0)
     def band_step(i, _):
         first = jnp.where(i == 0, 1.0, 0.0)
         last = jnp.where(i == step_count - 1, 1.0, 0.0)
@@ -306,7 +317,6 @@
         return 0
 
     lax.fori_loop(0, step_count, band_step, 0)
-    send_all(0)
     sort(1, other_half, blank, give)
     give_all(1)
 

time: 34.6 us -> 34.8 us (level)
  no operation moved by 1% of the time
where the time goes in v4:
time: 34.8 us; the launch traced here: 34.7 us
  Pallas kernels  34 us (98%)
  between operations  0.64 us (2%)
    pallas_call x1, Pallas kernels, per_device(): pl.pallas_call(functools.partial(exchange_kernel, n_fib, n_wav), out_shap...  33 us
    pallas_call x1, Pallas kernels, per_device(): pl.pallas_call(finish_kernel, out_shape=(jax.ShapeDtypeStruct((half, F_DE...  1.05 us

profile of v4, /device:TPU:1, one launch (start us, length us, event | category | flops | bytes accessed | tf_op | source)
XLA Modules:
  0.0 34.7 jit_solution(7818859527935700017)
XLA Ops:
  0.6 33.0 %exchange.1 = (bf16[256,256]{1,0:T(8,128)(2,1)S(1)}, f32[240,256]{1,0:T(8,128)S(1)}, f32[3,240,256]{2,1,0:T(8,128)S(1)}, f32[2,256,128]{2,1,0:T(8,128)S(1)}) custom-call(f32[4,480,256]{2,1,0:T(8,128)} %pix_hbm.1, f32[4,480,256]{2,1,0:T(8,128)} %ivar_hbm.1, s32[4,32,256]{2,1,0:T(8,128)} %bits_hbm.1, f32[2,128]{1,0:T(2,128)} %bitcast.4, s32[2,128]{1,0:T(2,128)} %bitcast.5, ...), custom_call_target="tpu_custom_call" | custom-call | tf_op jit(solution)/shard_map/exchange/pallas_call | solution.py:522
  33.6 1.0 %finish.1 = (f32[240,256]{1,0:T(8,128)}, f32[240,256]{1,0:T(8,128)}, f32[3,240,256]{2,1,0:T(8,128)}) custom-call(bf16[256,256]{1,0:T(8,128)(2,1)S(1)} %get-tuple-element.7.place_ref, f32[240,256]{1,0:T(8,128)S(1)} %get-tuple-element.8.ivar_ref, f32[3,240,256]{2,1,0:T(8,128)S(1)} %get-tuple-element.9.res_ref, f32[2,256,128]{2,1,0:T(8,128)S(1)} %get-tuple-element.10.got_ref), custom_call_target="tpu_custom_call" | custom-call | tf_op jit(solution)/shard_map/finish/pallas_call | solution.py:582
